TPU v7x, 256 devices: a whole 4x4x8 slice. The times are simulated.
256 devices in a mesh: seg: 8 (over x, y_hi), gx: 2 (over y_lo), gz: 16 (over z, core).
Axes of the slice: x: 4, y: 4 (y_hi: 2, y_lo: 2; y = y_hi * 2 + y_lo), z: 8, core: 2. Of those that a mesh axis runs over, the one named last changes fastest.
Arguments:
- terminal: float32 [8, 3, 128, 256, 256], P('seg', None, 'gx', 'gz'), may hold values from -6 to 6
- jump: float32 [8, 3, 128, 256, 256], P('seg', None, 'gx', 'gz'), may hold values from -61 to 61
- tangent: float32 [8, 3, 128, 256, 256], P('seg', None, 'gx', 'gz'), may hold values from -36 to 36
- base_velocity: float32 [256], replicated, may hold values from 0.5 to 2
- base_shear: float32 [256], replicated, may hold values from -2 to 2
Outputs:
- adjoint_field: float32 [8, 3, 128, 256, 256], P('seg', None, 'gx', 'gz')
All inputs are finite; a program needn't handle non-finite values. Where the computation divides by a largest or mean magnitude, that divisor is 1e-20 or more.
Results may differ from a plain program's by a relative error of at most 0.00018.
Values sent between devices are 32-bit elements; how exact they have to be, the bound alone decides.
A program may use at most 64 MiB of HBM per device.

v0:
```python
import jax
import jax.numpy as jnp
import numpy as np
from jax import lax
from jax.sharding import PartitionSpec as P

STEPS = 4
TIME_STEP = 0.15
DIFFUSE = 0.1
WALL_COEF = 0.0002
EPSILON = 1e-06
NEWTON_TURNS = 100


def with_halo(cells, sides, width):
    for axis, dim in sides:
        count = lax.axis_size(axis)
        head = lax.slice_in_dim(cells, 0, width, axis=dim)
        tail = lax.slice_in_dim(cells, cells.shape[dim] - width, cells.shape[dim], axis=dim)
        cells = jnp.concatenate(
            [
                lax.ppermute(tail, axis, [(i, (i + 1) % count) for i in range(count)]),
                cells,
                lax.ppermute(head, axis, [((i + 1) % count, i) for i in range(count)]),
            ],
            axis=dim,
        )
    return cells


def from_behind(value, axis, steps):
    count = lax.axis_size(axis)
    pairs = [(source, (source + steps) % count) for source in range(count)]
    return lax.ppermute(value, axis, pairs)


def invert_newton(matrix):
    order = matrix.shape[0]
    identity = np.eye(order)
    scale_one = np.max(np.sum(np.abs(matrix), axis=0))
    scale_inf = np.max(np.sum(np.abs(matrix), axis=1))
    approx = matrix.T / (scale_one * scale_inf)
    for turn_index in range(NEWTON_TURNS):
        approx = approx @ (2.0 * identity - matrix @ approx)
    return approx


def wall_table(points):
    intervals = points - 1
    cheb_nodes = np.cos(np.pi * np.arange(points) / intervals)
    weights = np.ones(points)
    weights[0] = 2.0
    weights[-1] = 2.0
    weights = weights * (-1.0) ** np.arange(points)
    spread = cheb_nodes[:, None] - cheb_nodes[None, :]
    first_deriv = weights[:, None] / weights[None, :] / (spread + np.eye(points))
    first_deriv = first_deriv - np.eye(points) * first_deriv.sum(axis=1)[:, None]
    second = first_deriv @ first_deriv
    interior = np.eye(points - 2) - WALL_COEF * second[1:-1, 1:-1]
    helm_table = np.zeros((points, points))
    helm_table[1:-1, 1:-1] = invert_newton(interior)
    return jnp.asarray(helm_table.T, dtype=jnp.float32)


def advance(padded, velocity, shear, table_t):
    center = padded[:, 2:-2, 2:-2, :]
    fwd2_x = padded[:, 4:, 2:-2, :]
    fwd1_x = padded[:, 3:-1, 2:-2, :]
    back1_x = padded[:, 1:-3, 2:-2, :]
    back2_x = padded[:, :-4, 2:-2, :]
    fwd2_z = padded[:, 2:-2, 4:, :]
    fwd1_z = padded[:, 2:-2, 3:-1, :]
    back1_z = padded[:, 2:-2, 1:-3, :]
    back2_z = padded[:, 2:-2, :-4, :]
    advect = (back2_x - fwd2_x + 8.0 * (fwd1_x - back1_x)) / 12.0
    lap_x = (16.0 * (fwd1_x + back1_x) - (fwd2_x + back2_x) - 30.0 * center) / 12.0
    lap_z = (16.0 * (fwd1_z + back1_z) - (fwd2_z + back2_z) - 30.0 * center) / 12.0
    explicit = center + TIME_STEP * velocity * advect + DIFFUSE * (lap_x + lap_z)
    explicit = jnp.concatenate(
        [explicit[:1], explicit[1:2] - TIME_STEP * shear * center[:1], explicit[2:]], axis=0
    )
    flattened = explicit.reshape(-1, explicit.shape[-1])
    updated = jnp.dot(
        flattened, table_t, precision=lax.Precision.HIGHEST, preferred_element_type=jnp.float32
    )
    return updated.reshape(explicit.shape)


def extend(adjoint, width):
    along_x = with_halo(adjoint, (("gx", 1),), width)
    return with_halo(along_x, (("gz", 2),), width)


def shards(terminal, jump, tangent, base_velocity, base_shear):
    table_t = wall_table(base_velocity.shape[0])
    received = from_behind(terminal, "seg", -1)
    started = received[0] + jump[0]
    direction = tangent[0]
    products = lax.psum(
        (jnp.sum(started * direction), jnp.sum(direction * direction)), ("gx", "gz")
    )
    along_coef = products[0] / (products[1] + EPSILON)
    adjoint = started - along_coef * direction
    for step_index in range(STEPS):
        padded = extend(adjoint, 2)
        adjoint = advance(padded, base_velocity, base_shear, table_t)
    return adjoint[None]


def solution(mesh):
    in_specs = (
        P("seg", None, "gx", "gz", None),
        P("seg", None, "gx", "gz", None),
        P("seg", None, "gx", "gz", None),
        P(),
        P(),
    )
    out_specs = P("seg", None, "gx", "gz", None)
    return jax.shard_map(shards, mesh=mesh, in_specs=in_specs, out_specs=out_specs, check_vma=False)
```

profile of v0, /device:TPU:22, one launch (start us, length us, event | category | flops | bytes accessed | tf_op | source)
XLA Modules:
  0.0 248.8 jit_solution(7663834592041668082)
XLA Ops:
  0.3 73.3 %collective-permute-done = f32[1,3,64,16,256]{4,3,2,1,0:T(8,128)S(1)} collective-permute-done((f32[1,3,64,16,256]{4,3,2,1,0:T(8,128)}, f32[1,3,64,16,256]{4,3,2,1,0:T(8,128)S(1)}, u32[]{:S(2)}, u32[]{:S(2)}) %collective-permute-start) | collective-permute-done | bytes 3145760 | tf_op jit(solution)/shard_map/ppermute | solution.py:34
  73.7 5.4 %fusion.39 = (f32[]{:T(128)}, f32[]{:T(128)}) fusion(f32[1,3,64,16,256]{4,3,2,1,0:T(8,128)} %param.8, f32[1,3,64,16,256]{4,3,2,1,0:T(8,128)S(1)} %collective-permute-done, f32[1,3,64,16,256]{4,3,2,1,0:T(8,128)} %param.7), kind=kLoop, calls=%fused_computation.85 | loop fusion | flops 3932158 | bytes 9437192 | tf_op jit(solution)/shard_map/reduce_sum | solution.py:100
  79.1 58.7 %all-reduce = (f32[]{:T(128)}, f32[]{:T(128)}) all-reduce(f32[]{:T(128)} %get-tuple-element.6, f32[]{:T(128)} %get-tuple-element.5), channel_id=1, replica_groups=mesh['seg'=8,'gx'=2,'gz'=16] {'gx','gz'}, use_global_device_ids=true, to_apply=%region_1.0 | all-reduce | flops 2 | bytes 16 | tf_op jit(solution)/shard_map/psum | solution.py:99
  139.2 4.0 %fusion.40 = f32[3,64,16,256]{3,2,1,0:T(8,128)S(1)} fusion(f32[1,3,64,16,256]{4,3,2,1,0:T(8,128)S(1)} %copy-done, f32[]{:T(128)S(6)} %div.31, f32[1,3,64,16,256]{4,3,2,1,0:T(8,128)} %copy-done.1, f32[1,3,64,16,256]{4,3,2,1,0:T(8,128)} %param.7), kind=kLoop, calls=%fused_computation.86 | loop fusion | flops 2359296 | bytes 12582916 | tf_op jit(solution)/shard_map/sub | solution.py:103
  145.3 2.6 %collective-permute-done.1 = f32[3,2,16,256]{3,2,1,0:T(8,128)S(1)} collective-permute-done((f32[3,2,16,256]{3,2,1,0:T(8,128)S(1)}, f32[3,2,16,256]{3,2,1,0:T(8,128)S(1)}, u32[]{:S(2)}, u32[]{:S(2)}) %collective-permute-start.1) | collective-permute-done | bytes 98336 | tf_op jit(solution)/shard_map/ppermute | solution.py:22
  149.8 5.0 %collective-permute-done.3 = f32[3,68,2,256]{3,2,1,0:T(2,128)S(1)} collective-permute-done((f32[3,68,2,256]{3,2,1,0:T(2,128)S(1)}, f32[3,68,2,256]{3,2,1,0:T(2,128)S(1)}, u32[]{:S(2)}, u32[]{:S(2)}) %collective-permute-start.3) | collective-permute-done | bytes 417824 | tf_op jit(solution)/shard_map/ppermute | solution.py:24
  154.8 3.1 %collective-permute-done.4 = f32[3,68,2,256]{3,2,1,0:T(2,128)S(1)} collective-permute-done((f32[3,68,2,256]{3,2,1,0:T(2,128)S(1)}, f32[3,68,2,256]{3,2,1,0:T(2,128)S(1)}, u32[]{:S(2)}, u32[]{:S(2)}) %collective-permute-start.4) | collective-permute-done | bytes 417824 | tf_op jit(solution)/shard_map/ppermute | solution.py:22
  159.3 4.1 %fusion.30 = f32[3,64,16,256]{3,2,1,0:T(8,128)} fusion(f32[3,68,18,256]{3,2,1,0:T(8,128)S(1)} %get-tuple-element.22, f32[3,68,18,256]{3,2,1,0:T(8,128)S(1)} %get-tuple-element.21, f32[3,64,16,256]{3,2,1,0:T(8,128)S(1)} %fusion.40, f32[3,2,16,256]{3,2,1,0:T(8,128)S(1)} %collective-permute-done.2, f32[3,2,16,256]{3,2,1,0:T(8,128)S(1)} %collective-permute-done.1, ...), kind=kLoop, calls=%fused_computation.67 | loop fusion | flops 18874368 | bytes 19072000 | tf_op jit(solution)/shard_map/add | solution.py:78
  166.7 2.6 %fusion.54 = f32[3072,256]{1,0:T(8,128)S(1)} fusion(f32[3072,256]{1,0:T(8,128)S(1)} %bitcast.47, f32[256,256]{1,0:T(8,128)S(1)} %copy-done.2), kind=kOutput, calls=%fused_computation.116 | convolution fusion | flops 2415919104 | bytes 6553600 | tf_op jit(solution)/shard_map/dot_general | solution.py:83
  171.4 2.6 %collective-permute-done.5 = f32[3,2,16,256]{3,2,1,0:T(8,128)S(1)} collective-permute-done((f32[3,2,16,256]{3,2,1,0:T(8,128)S(1)}, f32[3,2,16,256]{3,2,1,0:T(8,128)S(1)}, u32[]{:S(2)}, u32[]{:S(2)}) %collective-permute-start.5) | collective-permute-done | bytes 98336 | tf_op jit(solution)/shard_map/ppermute | solution.py:22
  176.0 5.0 %collective-permute-done.7 = f32[3,68,2,256]{3,2,1,0:T(2,128)S(1)} collective-permute-done((f32[3,68,2,256]{3,2,1,0:T(2,128)S(1)}, f32[3,68,2,256]{3,2,1,0:T(2,128)S(1)}, u32[]{:S(2)}, u32[]{:S(2)}) %collective-permute-start.7) | collective-permute-done | bytes 417824 | tf_op jit(solution)/shard_map/ppermute | solution.py:24
  181.0 3.1 %collective-permute-done.8 = f32[3,68,2,256]{3,2,1,0:T(2,128)S(1)} collective-permute-done((f32[3,68,2,256]{3,2,1,0:T(2,128)S(1)}, f32[3,68,2,256]{3,2,1,0:T(2,128)S(1)}, u32[]{:S(2)}, u32[]{:S(2)}) %collective-permute-start.8) | collective-permute-done | bytes 417824 | tf_op jit(solution)/shard_map/ppermute | solution.py:22
  185.4 5.0 %fusion.24 = f32[3,64,16,256]{3,2,1,0:T(8,128)} fusion(f32[3,68,18,256]{3,2,1,0:T(8,128)S(1)} %get-tuple-element.18, f32[3,68,18,256]{3,2,1,0:T(8,128)S(1)} %get-tuple-element.17, f32[3,64,16,256]{3,2,1,0:T(8,128)S(1)} %bitcast.41, f32[3,2,16,256]{3,2,1,0:T(8,128)} %copy-done.3, f32[3,2,16,256]{3,2,1,0:T(8,128)S(1)} %collective-permute-done.5, ...), kind=kLoop, calls=%fused_computation.57 | loop fusion | flops 18874368 | bytes 19072000 | tf_op jit(solution)/shard_map/add | solution.py:78
  193.0 2.6 %fusion.55 = f32[3072,256]{1,0:T(8,128)S(1)} fusion(f32[3072,256]{1,0:T(8,128)S(1)} %bitcast.48, f32[256,256]{1,0:T(8,128)S(1)} %copy-done.2), kind=kOutput, calls=%fused_computation.117 | convolution fusion | flops 2415919104 | bytes 6553600 | tf_op jit(solution)/shard_map/dot_general | solution.py:83
  197.8 2.6 %collective-permute-done.10 = f32[3,2,16,256]{3,2,1,0:T(8,128)S(1)} collective-permute-done((f32[3,2,16,256]{3,2,1,0:T(8,128)S(1)}, f32[3,2,16,256]{3,2,1,0:T(8,128)S(1)}, u32[]{:S(2)}, u32[]{:S(2)}) %collective-permute-start.10) | collective-permute-done | bytes 98336 | tf_op jit(solution)/shard_map/ppermute | solution.py:24
  202.3 5.0 %collective-permute-done.11 = f32[3,68,2,256]{3,2,1,0:T(2,128)S(1)} collective-permute-done((f32[3,68,2,256]{3,2,1,0:T(2,128)S(1)}, f32[3,68,2,256]{3,2,1,0:T(2,128)S(1)}, u32[]{:S(2)}, u32[]{:S(2)}) %collective-permute-start.11) | collective-permute-done | bytes 417824 | tf_op jit(solution)/shard_map/ppermute | solution.py:24
  207.3 3.1 %collective-permute-done.12 = f32[3,68,2,256]{3,2,1,0:T(2,128)S(1)} collective-permute-done((f32[3,68,2,256]{3,2,1,0:T(2,128)S(1)}, f32[3,68,2,256]{3,2,1,0:T(2,128)S(1)}, u32[]{:S(2)}, u32[]{:S(2)}) %collective-permute-start.12) | collective-permute-done | bytes 417824 | tf_op jit(solution)/shard_map/ppermute | solution.py:22
  211.8 4.9 %fusion.18 = f32[3,64,16,256]{3,2,1,0:T(8,128)} fusion(f32[3,68,18,256]{3,2,1,0:T(8,128)S(1)} %get-tuple-element.14, f32[3,68,18,256]{3,2,1,0:T(8,128)S(1)} %get-tuple-element.13, f32[3,64,16,256]{3,2,1,0:T(8,128)S(1)} %bitcast.45, f32[3,2,16,256]{3,2,1,0:T(8,128)S(1)} %collective-permute-done.10, f32[3,2,16,256]{3,2,1,0:T(8,128)} %copy-done.4, ...), kind=kLoop, calls=%fused_computation.47 | loop fusion | flops 18874368 | bytes 19072000 | tf_op jit(solution)/shard_map/add | solution.py:78
  219.3 2.6 %fusion.56 = f32[3072,256]{1,0:T(8,128)S(1)} fusion(f32[3072,256]{1,0:T(8,128)S(1)} %bitcast.46, f32[256,256]{1,0:T(8,128)S(1)} %copy-done.2), kind=kOutput, calls=%fused_computation.118 | convolution fusion | flops 2415919104 | bytes 6553600 | tf_op jit(solution)/shard_map/dot_general | solution.py:83
  224.1 2.6 %collective-permute-done.13 = f32[3,2,16,256]{3,2,1,0:T(8,128)S(1)} collective-permute-done((f32[3,2,16,256]{3,2,1,0:T(8,128)S(1)}, f32[3,2,16,256]{3,2,1,0:T(8,128)S(1)}, u32[]{:S(2)}, u32[]{:S(2)}) %collective-permute-start.13) | collective-permute-done | bytes 98336 | tf_op jit(solution)/shard_map/ppermute | solution.py:22
  228.6 5.0 %collective-permute-done.15 = f32[3,68,2,256]{3,2,1,0:T(2,128)S(1)} collective-permute-done((f32[3,68,2,256]{3,2,1,0:T(2,128)S(1)}, f32[3,68,2,256]{3,2,1,0:T(2,128)S(1)}, u32[]{:S(2)}, u32[]{:S(2)}) %collective-permute-start.15) | collective-permute-done | bytes 417824 | tf_op jit(solution)/shard_map/ppermute | solution.py:24
  233.6 3.1 %collective-permute-done.16 = f32[3,68,2,256]{3,2,1,0:T(2,128)S(1)} collective-permute-done((f32[3,68,2,256]{3,2,1,0:T(2,128)S(1)}, f32[3,68,2,256]{3,2,1,0:T(2,128)S(1)}, u32[]{:S(2)}, u32[]{:S(2)}) %collective-permute-start.16) | collective-permute-done | bytes 417824 | tf_op jit(solution)/shard_map/ppermute | solution.py:22
  238.0 4.1 %fusion.12 = f32[3,64,16,256]{3,2,1,0:T(8,128)} fusion(f32[3,68,18,256]{3,2,1,0:T(8,128)S(1)} %get-tuple-element.10, f32[3,68,18,256]{3,2,1,0:T(8,128)S(1)} %get-tuple-element.9, f32[3,64,16,256]{3,2,1,0:T(8,128)S(1)} %bitcast.37, f32[3,2,16,256]{3,2,1,0:T(8,128)S(1)} %collective-permute-done.14, f32[3,2,16,256]{3,2,1,0:T(8,128)S(1)} %collective-permute-done.13, ...), kind=kLoop, calls=%fused_computation.37 | loop fusion | flops 18874368 | bytes 19072000 | tf_op jit(solution)/shard_map/add | solution.py:78
  244.5 4.3 %fusion.41 = f32[1,3,64,16,256]{4,3,2,1,0:T(8,128)} fusion(f32[256,256,1,1]{1,0,3,2:T(8,128)S(1)} %copy-done.5, f32[1,64,16,256]{3,2,1,0:T(8,128)S(1)} %get-tuple-element.26, f32[1,64,16,256]{3,2,1,0:T(8,128)S(1)} %get-tuple-element.27, f32[1,64,16,256]{3,2,1,0:T(8,128)S(1)} %get-tuple-element.25), kind=kOutput, calls=%fused_computation.87 | convolution fusion | flops 2417491968 | bytes 6553600 | tf_op jit(solution)/shard_map/dot_general | solution.py:83
  (61 shorter events, 32.6 us)
Async XLA Ops:
  0.0 139.1 %copy-start = (f32[1,3,64,16,256]{4,3,2,1,0:T(8,128)S(1)}, f32[1,3,64,16,256]{4,3,2,1,0:T(8,128)}, u32[]{:S(2)}) copy-start(f32[1,3,64,16,256]{4,3,2,1,0:T(8,128)} %param.8) | copy-start | bytes 9437188
  0.0 73.7 %collective-permute-start = (f32[1,3,64,16,256]{4,3,2,1,0:T(8,128)}, f32[1,3,64,16,256]{4,3,2,1,0:T(8,128)S(1)}, u32[]{:S(2)}, u32[]{:S(2)}) collective-permute-start(f32[1,3,64,16,256]{4,3,2,1,0:T(8,128)} %param.6), channel_id=1, source_target_pairs={{0,224},{32,0},{64,32},{96,64},{128,96},{160,128},{192,160},{224,1... | collective-permute-start | bytes 9437192 | tf_op jit(solution)/shard_map/ppermute | solution.py:34
  73.7 5.4 %copy-start.1 = (f32[1,3,64,16,256]{4,3,2,1,0:T(8,128)}, f32[1,3,64,16,256]{4,3,2,1,0:T(8,128)S(1)}, u32[]{:S(2)}) copy-start(f32[1,3,64,16,256]{4,3,2,1,0:T(8,128)S(1)} %collective-permute-done) | copy-start | bytes 9437188
  143.2 6.6 %copy-start.6 = (f32[256]{0:T(256)S(1)}, f32[256]{0:T(256)}, u32[]{:S(2)}) copy-start(f32[256]{0:T(256)} %param.9) | copy-start | bytes 3076
  143.2 6.6 %copy-start.7 = (f32[256]{0:T(256)S(1)}, f32[256]{0:T(256)}, u32[]{:S(2)}) copy-start(f32[256]{0:T(256)} %param.10) | copy-start | bytes 3076
  143.2 4.7 %collective-permute-start.1 = (f32[3,2,16,256]{3,2,1,0:T(8,128)S(1)}, f32[3,2,16,256]{3,2,1,0:T(8,128)S(1)}, u32[]{:S(2)}, u32[]{:S(2)}) collective-permute-start(f32[3,2,16,256]{3,2,1,0:T(8,128)S(1)} %get-tuple-element.43), channel_id=1, source_target_pairs={{0,16},{16,0},{1,17},{17,1},{2,18},{18,2},{3,19},{19,3},{4,20},{20... | collective-permute-start | bytes 294920 | tf_op jit(solution)/shard_map/ppermute | solution.py:22
  144.0 4.9 %collective-permute-start.2 = (f32[3,2,16,256]{3,2,1,0:T(8,128)S(1)}, f32[3,2,16,256]{3,2,1,0:T(8,128)S(1)}, u32[]{:S(2)}, u32[]{:S(2)}) collective-permute-start(f32[3,2,16,256]{3,2,1,0:T(8,128)S(1)} %get-tuple-element.44), channel_id=1, source_target_pairs={{16,0},{0,16},{17,1},{1,17},{18,2},{2,18},{19,3},{3,19},{20,4},{4,... | collective-permute-start | bytes 294920 | tf_op jit(solution)/shard_map/ppermute | solution.py:24
  149.3 5.6 %collective-permute-start.3 = (f32[3,68,2,256]{3,2,1,0:T(2,128)S(1)}, f32[3,68,2,256]{3,2,1,0:T(2,128)S(1)}, u32[]{:S(2)}, u32[]{:S(2)}) collective-permute-start(f32[3,68,2,256]{3,2,1,0:T(2,128)S(1)} %get-tuple-element.23), channel_id=1, source_target_pairs={{1,0},{2,1},{3,2},{4,3},{5,4},{6,5},{7,6},{8,7},{9,8},{10,9},{11,1... | collective-permute-start | bytes 1253384 | tf_op jit(solution)/shard_map/ppermute | solution.py:24
  149.3 8.7 %collective-permute-start.4 = (f32[3,68,2,256]{3,2,1,0:T(2,128)S(1)}, f32[3,68,2,256]{3,2,1,0:T(2,128)S(1)}, u32[]{:S(2)}, u32[]{:S(2)}) collective-permute-start(f32[3,68,2,256]{3,2,1,0:T(2,128)S(1)} %get-tuple-element.24), channel_id=1, source_target_pairs={{0,1},{1,2},{2,3},{3,4},{4,5},{5,6},{6,7},{7,8},{8,9},{9,10},{10,1... | collective-permute-start | bytes 1253384 | tf_op jit(solution)/shard_map/ppermute | solution.py:22
  169.3 4.7 %collective-permute-start.5 = (f32[3,2,16,256]{3,2,1,0:T(8,128)S(1)}, f32[3,2,16,256]{3,2,1,0:T(8,128)S(1)}, u32[]{:S(2)}, u32[]{:S(2)}) collective-permute-start(f32[3,2,16,256]{3,2,1,0:T(8,128)S(1)} %get-tuple-element.38), channel_id=1, source_target_pairs={{0,16},{16,0},{1,17},{17,1},{2,18},{18,2},{3,19},{19,3},{4,20},{20... | collective-permute-start | bytes 294920 | tf_op jit(solution)/shard_map/ppermute | solution.py:22
  170.4 4.7 %collective-permute-start.6 = (f32[3,2,16,256]{3,2,1,0:T(8,128)S(1)}, f32[3,2,16,256]{3,2,1,0:T(8,128)S(1)}, u32[]{:S(2)}, u32[]{:S(2)}) collective-permute-start(f32[3,2,16,256]{3,2,1,0:T(8,128)S(1)} %get-tuple-element.39), channel_id=1, source_target_pairs={{16,0},{0,16},{17,1},{1,17},{18,2},{2,18},{19,3},{3,19},{20,4},{4,... | collective-permute-start | bytes 294920 | tf_op jit(solution)/shard_map/ppermute | solution.py:24
  175.1 10.3 %copy-start.3 = (f32[3,2,16,256]{3,2,1,0:T(8,128)}, f32[3,2,16,256]{3,2,1,0:T(8,128)S(1)}, u32[]{:S(2)}) copy-start(f32[3,2,16,256]{3,2,1,0:T(8,128)S(1)} %collective-permute-done.6) | copy-start | bytes 294916
  175.4 5.6 %collective-permute-start.7 = (f32[3,68,2,256]{3,2,1,0:T(2,128)S(1)}, f32[3,68,2,256]{3,2,1,0:T(2,128)S(1)}, u32[]{:S(2)}, u32[]{:S(2)}) collective-permute-start(f32[3,68,2,256]{3,2,1,0:T(2,128)S(1)} %get-tuple-element.19), channel_id=1, source_target_pairs={{1,0},{2,1},{3,2},{4,3},{5,4},{6,5},{7,6},{8,7},{9,8},{10,9},{11,1... | collective-permute-start | bytes 1253384 | tf_op jit(solution)/shard_map/ppermute | solution.py:24
  175.4 8.7 %collective-permute-start.8 = (f32[3,68,2,256]{3,2,1,0:T(2,128)S(1)}, f32[3,68,2,256]{3,2,1,0:T(2,128)S(1)}, u32[]{:S(2)}, u32[]{:S(2)}) collective-permute-start(f32[3,68,2,256]{3,2,1,0:T(2,128)S(1)} %get-tuple-element.20), channel_id=1, source_target_pairs={{0,1},{1,2},{2,3},{3,4},{4,5},{5,6},{6,7},{7,8},{8,9},{9,10},{10,1... | collective-permute-start | bytes 1253384 | tf_op jit(solution)/shard_map/ppermute | solution.py:22
  195.7 4.7 %collective-permute-start.10 = (f32[3,2,16,256]{3,2,1,0:T(8,128)S(1)}, f32[3,2,16,256]{3,2,1,0:T(8,128)S(1)}, u32[]{:S(2)}, u32[]{:S(2)}) collective-permute-start(f32[3,2,16,256]{3,2,1,0:T(8,128)S(1)} %get-tuple-element.34), channel_id=1, source_target_pairs={{16,0},{0,16},{17,1},{1,17},{18,2},{2,18},{19,3},{3,19},{20,4},{4,... | collective-permute-start | bytes 294920 | tf_op jit(solution)/shard_map/ppermute | solution.py:24
  196.8 4.7 %collective-permute-start.9 = (f32[3,2,16,256]{3,2,1,0:T(8,128)S(1)}, f32[3,2,16,256]{3,2,1,0:T(8,128)S(1)}, u32[]{:S(2)}, u32[]{:S(2)}) collective-permute-start(f32[3,2,16,256]{3,2,1,0:T(8,128)S(1)} %get-tuple-element.33), channel_id=1, source_target_pairs={{0,16},{16,0},{1,17},{17,1},{2,18},{18,2},{3,19},{19,3},{4,20},{20... | collective-permute-start | bytes 294920 | tf_op jit(solution)/shard_map/ppermute | solution.py:22
  201.4 10.3 %copy-start.4 = (f32[3,2,16,256]{3,2,1,0:T(8,128)}, f32[3,2,16,256]{3,2,1,0:T(8,128)S(1)}, u32[]{:S(2)}) copy-start(f32[3,2,16,256]{3,2,1,0:T(8,128)S(1)} %collective-permute-done.9) | copy-start | bytes 294916
  201.7 5.6 %collective-permute-start.11 = (f32[3,68,2,256]{3,2,1,0:T(2,128)S(1)}, f32[3,68,2,256]{3,2,1,0:T(2,128)S(1)}, u32[]{:S(2)}, u32[]{:S(2)}) collective-permute-start(f32[3,68,2,256]{3,2,1,0:T(2,128)S(1)} %get-tuple-element.15), channel_id=1, source_target_pairs={{1,0},{2,1},{3,2},{4,3},{5,4},{6,5},{7,6},{8,7},{9,8},{10,9},{11,1... | collective-permute-start | bytes 1253384 | tf_op jit(solution)/shard_map/ppermute | solution.py:24
  201.8 8.7 %collective-permute-start.12 = (f32[3,68,2,256]{3,2,1,0:T(2,128)S(1)}, f32[3,68,2,256]{3,2,1,0:T(2,128)S(1)}, u32[]{:S(2)}, u32[]{:S(2)}) collective-permute-start(f32[3,68,2,256]{3,2,1,0:T(2,128)S(1)} %get-tuple-element.16), channel_id=1, source_target_pairs={{0,1},{1,2},{2,3},{3,4},{4,5},{5,6},{6,7},{7,8},{8,9},{9,10},{10,1... | collective-permute-start | bytes 1253384 | tf_op jit(solution)/shard_map/ppermute | solution.py:22
  221.9 4.7 %collective-permute-start.13 = (f32[3,2,16,256]{3,2,1,0:T(8,128)S(1)}, f32[3,2,16,256]{3,2,1,0:T(8,128)S(1)}, u32[]{:S(2)}, u32[]{:S(2)}) collective-permute-start(f32[3,2,16,256]{3,2,1,0:T(8,128)S(1)} %get-tuple-element.28), channel_id=1, source_target_pairs={{0,16},{16,0},{1,17},{17,1},{2,18},{18,2},{3,19},{19,3},{4,20},{20... | collective-permute-start | bytes 294920 | tf_op jit(solution)/shard_map/ppermute | solution.py:22
  223.0 4.7 %collective-permute-start.14 = (f32[3,2,16,256]{3,2,1,0:T(8,128)S(1)}, f32[3,2,16,256]{3,2,1,0:T(8,128)S(1)}, u32[]{:S(2)}, u32[]{:S(2)}) collective-permute-start(f32[3,2,16,256]{3,2,1,0:T(8,128)S(1)} %get-tuple-element.29), channel_id=1, source_target_pairs={{16,0},{0,16},{17,1},{1,17},{18,2},{2,18},{19,3},{3,19},{20,4},{4,... | collective-permute-start | bytes 294920 | tf_op jit(solution)/shard_map/ppermute | solution.py:24
  228.0 5.6 %collective-permute-start.15 = (f32[3,68,2,256]{3,2,1,0:T(2,128)S(1)}, f32[3,68,2,256]{3,2,1,0:T(2,128)S(1)}, u32[]{:S(2)}, u32[]{:S(2)}) collective-permute-start(f32[3,68,2,256]{3,2,1,0:T(2,128)S(1)} %get-tuple-element.11), channel_id=1, source_target_pairs={{1,0},{2,1},{3,2},{4,3},{5,4},{6,5},{7,6},{8,7},{9,8},{10,9},{11,1... | collective-permute-start | bytes 1253384 | tf_op jit(solution)/shard_map/ppermute | solution.py:24
  228.0 8.7 %collective-permute-start.16 = (f32[3,68,2,256]{3,2,1,0:T(2,128)S(1)}, f32[3,68,2,256]{3,2,1,0:T(2,128)S(1)}, u32[]{:S(2)}, u32[]{:S(2)}) collective-permute-start(f32[3,68,2,256]{3,2,1,0:T(2,128)S(1)} %get-tuple-element.12), channel_id=1, source_target_pairs={{0,1},{1,2},{2,3},{3,4},{4,5},{5,6},{6,7},{7,8},{8,9},{9,10},{10,1... | collective-permute-start | bytes 1253384 | tf_op jit(solution)/shard_map/ppermute | solution.py:22
  242.1 2.4 copy-start.5
  (1 other events, 1.0 us)
where the time goes:
time: 249 us
  waiting for transfers between devices  120 us (48%)
  blocking collectives  58.7 us (24%)
  other arithmetic  44.1 us (18%)
  matrix products  12.1 us (5%)
  starting transfers between devices  10.8 us (4%)
    ppermute x1, waiting for transfers between devices, from_behind(): return lax.ppermute(value, axis, pairs)  73.3 us
    psum x1, blocking collectives, shards(): lax.psum((jnp.sum(started * direction), jnp.sum(direction * direction)),...  58.7 us
    ppermute x8, waiting for transfers between devices, with_halo(): lax.ppermute(head, axis, [((i + 1) % count, i) for i in range(count)])  25.7 us
    ppermute x8, waiting for transfers between devices, with_halo(): lax.ppermute(tail, axis, [(i, (i + 1) % count) for i in range(count)])  21.4 us
    add x4, other arithmetic, advance(): center + TIME_STEP * velocity * advect + DIFFUSE * (lap_x + lap_z)  18 us
    dot_general x4, matrix products, advance(): jnp.dot(flattened, table_t, precision=lax.Precision.HIGHEST, preferred_el...  12.1 us
    slice x4, other arithmetic, advance(): explicit[:1]  9.38 us
    ppermute x8, starting transfers between devices, with_halo(): lax.ppermute(tail, axis, [(i, (i + 1) % count) for i in range(count)])  5.99 us
  transfers between devices with their start and end apart: 17, of which 17 were waited for; matrix products, arithmetic and copies ran while one was open for 0% of the time, Pallas kernels for 0%

commit v1 on v0

--- a/solution.py
+++ b/solution.py
@@ -96,9 +96,8 @@
     received = from_behind(terminal, "seg", -1)
     started = received[0] + jump[0]
     direction = tangent[0]
-    products = lax.psum(
-        (jnp.sum(started * direction), jnp.sum(direction * direction)), ("gx", "gz")
-    )
+    inner = lax.psum((jnp.sum(started * direction), jnp.sum(direction * direction)), "gz")
+    products = lax.psum(inner, "gx")
     along_coef = products[0] / (products[1] + EPSILON)
     adjoint = started - along_coef * direction
     for step_index in range(STEPS):

time: 249 us -> 225 us (0.904)
  blocking collectives: 58.7 us -> 34.2 us
    psum x1, blocking collectives: 58.7 us -> 28.6 us  [shards(): lax.psum((jnp.sum(started * direction), jnp.sum(direction * direction)),...]
    psum x0 -> x1, blocking collectives: none -> 5.58 us  [shards(): products = lax.psum(inner, 'gx')]
where the time goes in v1:
time: 225 us
  waiting for transfers between devices  121 us (54%)
  other arithmetic  44.1 us (20%)
  blocking collectives  34.2 us (15%)
  matrix products  12.1 us (5%)
  starting transfers between devices  10.8 us (5%)
    ppermute x1, waiting for transfers between devices, from_behind(): return lax.ppermute(value, axis, pairs)  73.3 us
    psum x1, blocking collectives, shards(): lax.psum((jnp.sum(started * direction), jnp.sum(direction * direction)),...  28.6 us
    ppermute x8, waiting for transfers between devices, with_halo(): lax.ppermute(head, axis, [((i + 1) % count, i) for i in range(count)])  26.2 us
    ppermute x8, waiting for transfers between devices, with_halo(): lax.ppermute(tail, axis, [(i, (i + 1) % count) for i in range(count)])  21.5 us
    add x4, other arithmetic, advance(): center + TIME_STEP * velocity * advect + DIFFUSE * (lap_x + lap_z)  18 us
    dot_general x4, matrix products, advance(): jnp.dot(flattened, table_t, precision=lax.Precision.HIGHEST, preferred_el...  12.1 us
    slice x4, other arithmetic, advance(): explicit[:1]  9.38 us
    ppermute x8, starting transfers between devices, with_halo(): lax.ppermute(tail, axis, [(i, (i + 1) % count) for i in range(count)])  6.64 us
  transfers between devices with their start and end apart: 17, of which 17 were waited for; matrix products, arithmetic and copies ran while one was open for 0% of the time, Pallas kernels for 0%

profile of v1, /device:TPU:22, one launch (start us, length us, event | category | flops | bytes accessed | tf_op | source)
XLA Modules:
  0.0 224.7 jit_solution(7545264665241350106)
XLA Ops:
  0.3 73.3 %collective-permute-done = f32[1,3,64,16,256]{4,3,2,1,0:T(8,128)S(1)} collective-permute-done((f32[1,3,64,16,256]{4,3,2,1,0:T(8,128)}, f32[1,3,64,16,256]{4,3,2,1,0:T(8,128)S(1)}, u32[]{:S(2)}, u32[]{:S(2)}) %collective-permute-start) | collective-permute-done | bytes 3145760 | tf_op jit(solution)/shard_map/ppermute | solution.py:34
  73.7 5.4 %fusion.39 = (f32[]{:T(128)}, f32[]{:T(128)}) fusion(f32[1,3,64,16,256]{4,3,2,1,0:T(8,128)} %param.8, f32[1,3,64,16,256]{4,3,2,1,0:T(8,128)S(1)} %collective-permute-done, f32[1,3,64,16,256]{4,3,2,1,0:T(8,128)} %param.7), kind=kLoop, calls=%fused_computation.85 | loop fusion | flops 3932158 | bytes 9437192 | tf_op jit(solution)/shard_map/reduce_sum | solution.py:99
  79.1 28.6 %all-reduce = (f32[]{:T(128)}, f32[]{:T(128)}) all-reduce(f32[]{:T(128)} %get-tuple-element.6, f32[]{:T(128)} %get-tuple-element.5), channel_id=1, replica_groups=mesh['seg'=8,'gx'=2,'gz'=16] {'gz'}, use_global_device_ids=true, to_apply=%region_1.0 | all-reduce | flops 2 | bytes 16 | tf_op jit(solution)/shard_map/psum | solution.py:99
  107.7 5.6 %all-reduce.1 = (f32[]{:T(128)}, f32[]{:T(128)}) all-reduce(f32[]{:T(128)} %get-tuple-element.7, f32[]{:T(128)} %get-tuple-element.8), channel_id=1, replica_groups=mesh['seg'=8,'gx'=2,'gz'=16] {'gx'}, use_global_device_ids=true, to_apply=%region_2.0 | all-reduce | flops 2 | bytes 16 | tf_op jit(solution)/shard_map/psum | solution.py:100
  114.5 4.0 %fusion.40 = f32[3,64,16,256]{3,2,1,0:T(8,128)S(1)} fusion(f32[1,3,64,16,256]{4,3,2,1,0:T(8,128)S(1)} %copy-done, f32[]{:T(128)S(6)} %div.31, f32[1,3,64,16,256]{4,3,2,1,0:T(8,128)} %copy-done.1, f32[1,3,64,16,256]{4,3,2,1,0:T(8,128)} %param.7), kind=kLoop, calls=%fused_computation.86 | loop fusion | flops 2359296 | bytes 12582916 | tf_op jit(solution)/shard_map/sub | solution.py:102
  120.7 2.6 %collective-permute-done.1 = f32[3,2,16,256]{3,2,1,0:T(8,128)S(1)} collective-permute-done((f32[3,2,16,256]{3,2,1,0:T(8,128)S(1)}, f32[3,2,16,256]{3,2,1,0:T(8,128)S(1)}, u32[]{:S(2)}, u32[]{:S(2)}) %collective-permute-start.1) | collective-permute-done | bytes 98336 | tf_op jit(solution)/shard_map/ppermute | solution.py:22
  125.4 5.0 %collective-permute-done.3 = f32[3,68,2,256]{3,2,1,0:T(2,128)S(1)} collective-permute-done((f32[3,68,2,256]{3,2,1,0:T(2,128)S(1)}, f32[3,68,2,256]{3,2,1,0:T(2,128)S(1)}, u32[]{:S(2)}, u32[]{:S(2)}) %collective-permute-start.3) | collective-permute-done | bytes 417824 | tf_op jit(solution)/shard_map/ppermute | solution.py:24
  130.4 3.1 %collective-permute-done.4 = f32[3,68,2,256]{3,2,1,0:T(2,128)S(1)} collective-permute-done((f32[3,68,2,256]{3,2,1,0:T(2,128)S(1)}, f32[3,68,2,256]{3,2,1,0:T(2,128)S(1)}, u32[]{:S(2)}, u32[]{:S(2)}) %collective-permute-start.4) | collective-permute-done | bytes 417824 | tf_op jit(solution)/shard_map/ppermute | solution.py:22
  134.9 4.1 %fusion.30 = f32[3,64,16,256]{3,2,1,0:T(8,128)} fusion(f32[3,68,18,256]{3,2,1,0:T(8,128)S(1)} %get-tuple-element.24, f32[3,68,18,256]{3,2,1,0:T(8,128)S(1)} %get-tuple-element.23, f32[3,64,16,256]{3,2,1,0:T(8,128)S(1)} %fusion.40, f32[3,2,16,256]{3,2,1,0:T(8,128)S(1)} %collective-permute-done.2, f32[3,2,16,256]{3,2,1,0:T(8,128)S(1)} %collective-permute-done.1, ...), kind=kLoop, calls=%fused_computation.67 | loop fusion | flops 18874368 | bytes 19072000 | tf_op jit(solution)/shard_map/add | solution.py:78
  142.3 2.6 %fusion.54 = f32[3072,256]{1,0:T(8,128)S(1)} fusion(f32[3072,256]{1,0:T(8,128)S(1)} %bitcast.47, f32[256,256]{1,0:T(8,128)S(1)} %copy-done.2), kind=kOutput, calls=%fused_computation.116 | convolution fusion | flops 2415919104 | bytes 6553600 | tf_op jit(solution)/shard_map/dot_general | solution.py:83
  147.0 2.6 %collective-permute-done.5 = f32[3,2,16,256]{3,2,1,0:T(8,128)S(1)} collective-permute-done((f32[3,2,16,256]{3,2,1,0:T(8,128)S(1)}, f32[3,2,16,256]{3,2,1,0:T(8,128)S(1)}, u32[]{:S(2)}, u32[]{:S(2)}) %collective-permute-start.5) | collective-permute-done | bytes 98336 | tf_op jit(solution)/shard_map/ppermute | solution.py:22
  151.6 5.0 %collective-permute-done.7 = f32[3,68,2,256]{3,2,1,0:T(2,128)S(1)} collective-permute-done((f32[3,68,2,256]{3,2,1,0:T(2,128)S(1)}, f32[3,68,2,256]{3,2,1,0:T(2,128)S(1)}, u32[]{:S(2)}, u32[]{:S(2)}) %collective-permute-start.7) | collective-permute-done | bytes 417824 | tf_op jit(solution)/shard_map/ppermute | solution.py:24
  156.6 3.1 %collective-permute-done.8 = f32[3,68,2,256]{3,2,1,0:T(2,128)S(1)} collective-permute-done((f32[3,68,2,256]{3,2,1,0:T(2,128)S(1)}, f32[3,68,2,256]{3,2,1,0:T(2,128)S(1)}, u32[]{:S(2)}, u32[]{:S(2)}) %collective-permute-start.8) | collective-permute-done | bytes 417824 | tf_op jit(solution)/shard_map/ppermute | solution.py:22
  161.0 5.0 %fusion.24 = f32[3,64,16,256]{3,2,1,0:T(8,128)} fusion(f32[3,68,18,256]{3,2,1,0:T(8,128)S(1)} %get-tuple-element.20, f32[3,68,18,256]{3,2,1,0:T(8,128)S(1)} %get-tuple-element.19, f32[3,64,16,256]{3,2,1,0:T(8,128)S(1)} %bitcast.41, f32[3,2,16,256]{3,2,1,0:T(8,128)} %copy-done.3, f32[3,2,16,256]{3,2,1,0:T(8,128)S(1)} %collective-permute-done.5, ...), kind=kLoop, calls=%fused_computation.57 | loop fusion | flops 18874368 | bytes 19072000 | tf_op jit(solution)/shard_map/add | solution.py:78
  168.6 2.6 %fusion.55 = f32[3072,256]{1,0:T(8,128)S(1)} fusion(f32[3072,256]{1,0:T(8,128)S(1)} %bitcast.48, f32[256,256]{1,0:T(8,128)S(1)} %copy-done.2), kind=kOutput, calls=%fused_computation.117 | convolution fusion | flops 2415919104 | bytes 6553600 | tf_op jit(solution)/shard_map/dot_general | solution.py:83
  178.1 5.0 %collective-permute-done.11 = f32[3,68,2,256]{3,2,1,0:T(2,128)S(1)} collective-permute-done((f32[3,68,2,256]{3,2,1,0:T(2,128)S(1)}, f32[3,68,2,256]{3,2,1,0:T(2,128)S(1)}, u32[]{:S(2)}, u32[]{:S(2)}) %collective-permute-start.11) | collective-permute-done | bytes 417824 | tf_op jit(solution)/shard_map/ppermute | solution.py:24
  183.1 3.1 %collective-permute-done.12 = f32[3,68,2,256]{3,2,1,0:T(2,128)S(1)} collective-permute-done((f32[3,68,2,256]{3,2,1,0:T(2,128)S(1)}, f32[3,68,2,256]{3,2,1,0:T(2,128)S(1)}, u32[]{:S(2)}, u32[]{:S(2)}) %collective-permute-start.12) | collective-permute-done | bytes 417824 | tf_op jit(solution)/shard_map/ppermute | solution.py:22
  187.5 4.9 %fusion.18 = f32[3,64,16,256]{3,2,1,0:T(8,128)} fusion(f32[3,68,18,256]{3,2,1,0:T(8,128)S(1)} %get-tuple-element.16, f32[3,68,18,256]{3,2,1,0:T(8,128)S(1)} %get-tuple-element.15, f32[3,64,16,256]{3,2,1,0:T(8,128)S(1)} %bitcast.45, f32[3,2,16,256]{3,2,1,0:T(8,128)S(1)} %collective-permute-done.10, f32[3,2,16,256]{3,2,1,0:T(8,128)} %copy-done.4, ...), kind=kLoop, calls=%fused_computation.47 | loop fusion | flops 18874368 | bytes 19072000 | tf_op jit(solution)/shard_map/add | solution.py:78
  195.1 2.6 %fusion.56 = f32[3072,256]{1,0:T(8,128)S(1)} fusion(f32[3072,256]{1,0:T(8,128)S(1)} %bitcast.46, f32[256,256]{1,0:T(8,128)S(1)} %copy-done.2), kind=kOutput, calls=%fused_computation.118 | convolution fusion | flops 2415919104 | bytes 6553600 | tf_op jit(solution)/shard_map/dot_general | solution.py:83
  199.8 2.6 %collective-permute-done.13 = f32[3,2,16,256]{3,2,1,0:T(8,128)S(1)} collective-permute-done((f32[3,2,16,256]{3,2,1,0:T(8,128)S(1)}, f32[3,2,16,256]{3,2,1,0:T(8,128)S(1)}, u32[]{:S(2)}, u32[]{:S(2)}) %collective-permute-start.13) | collective-permute-done | bytes 98336 | tf_op jit(solution)/shard_map/ppermute | solution.py:22
  204.5 5.0 %collective-permute-done.15 = f32[3,68,2,256]{3,2,1,0:T(2,128)S(1)} collective-permute-done((f32[3,68,2,256]{3,2,1,0:T(2,128)S(1)}, f32[3,68,2,256]{3,2,1,0:T(2,128)S(1)}, u32[]{:S(2)}, u32[]{:S(2)}) %collective-permute-start.15) | collective-permute-done | bytes 417824 | tf_op jit(solution)/shard_map/ppermute | solution.py:24
  209.5 3.1 %collective-permute-done.16 = f32[3,68,2,256]{3,2,1,0:T(2,128)S(1)} collective-permute-done((f32[3,68,2,256]{3,2,1,0:T(2,128)S(1)}, f32[3,68,2,256]{3,2,1,0:T(2,128)S(1)}, u32[]{:S(2)}, u32[]{:S(2)}) %collective-permute-start.16) | collective-permute-done | bytes 417824 | tf_op jit(solution)/shard_map/ppermute | solution.py:22
  214.0 4.1 %fusion.12 = f32[3,64,16,256]{3,2,1,0:T(8,128)} fusion(f32[3,68,18,256]{3,2,1,0:T(8,128)S(1)} %get-tuple-element.12, f32[3,68,18,256]{3,2,1,0:T(8,128)S(1)} %get-tuple-element.11, f32[3,64,16,256]{3,2,1,0:T(8,128)S(1)} %bitcast.37, f32[3,2,16,256]{3,2,1,0:T(8,128)S(1)} %collective-permute-done.14, f32[3,2,16,256]{3,2,1,0:T(8,128)S(1)} %collective-permute-done.13, ...), kind=kLoop, calls=%fused_computation.37 | loop fusion | flops 18874368 | bytes 19072000 | tf_op jit(solution)/shard_map/add | solution.py:78
  220.5 4.3 %fusion.41 = f32[1,3,64,16,256]{4,3,2,1,0:T(8,128)} fusion(f32[256,256,1,1]{1,0,3,2:T(8,128)S(1)} %copy-done.5, f32[1,64,16,256]{3,2,1,0:T(8,128)S(1)} %get-tuple-element.28, f32[1,64,16,256]{3,2,1,0:T(8,128)S(1)} %get-tuple-element.29, f32[1,64,16,256]{3,2,1,0:T(8,128)S(1)} %get-tuple-element.27), kind=kOutput, calls=%fused_computation.87 | convolution fusion | flops 2417491968 | bytes 6553600 | tf_op jit(solution)/shard_map/dot_general | solution.py:83
  (62 shorter events, 35.8 us)
Async XLA Ops:
  0.0 114.5 %copy-start = (f32[1,3,64,16,256]{4,3,2,1,0:T(8,128)S(1)}, f32[1,3,64,16,256]{4,3,2,1,0:T(8,128)}, u32[]{:S(2)}) copy-start(f32[1,3,64,16,256]{4,3,2,1,0:T(8,128)} %param.8) | copy-start | bytes 9437188
  0.0 73.7 %collective-permute-start = (f32[1,3,64,16,256]{4,3,2,1,0:T(8,128)}, f32[1,3,64,16,256]{4,3,2,1,0:T(8,128)S(1)}, u32[]{:S(2)}, u32[]{:S(2)}) collective-permute-start(f32[1,3,64,16,256]{4,3,2,1,0:T(8,128)} %param.6), channel_id=1, source_target_pairs={{0,224},{32,0},{64,32},{96,64},{128,96},{160,128},{192,160},{224,1... | collective-permute-start | bytes 9437192 | tf_op jit(solution)/shard_map/ppermute | solution.py:34
  73.7 5.4 %copy-start.1 = (f32[1,3,64,16,256]{4,3,2,1,0:T(8,128)}, f32[1,3,64,16,256]{4,3,2,1,0:T(8,128)S(1)}, u32[]{:S(2)}) copy-start(f32[1,3,64,16,256]{4,3,2,1,0:T(8,128)S(1)} %collective-permute-done) | copy-start | bytes 9437188
  118.5 6.9 %copy-start.6 = (f32[256]{0:T(256)S(1)}, f32[256]{0:T(256)}, u32[]{:S(2)}) copy-start(f32[256]{0:T(256)} %param.9) | copy-start | bytes 3076
  118.5 6.9 %copy-start.7 = (f32[256]{0:T(256)S(1)}, f32[256]{0:T(256)}, u32[]{:S(2)}) copy-start(f32[256]{0:T(256)} %param.10) | copy-start | bytes 3076
  118.6 4.7 %collective-permute-start.1 = (f32[3,2,16,256]{3,2,1,0:T(8,128)S(1)}, f32[3,2,16,256]{3,2,1,0:T(8,128)S(1)}, u32[]{:S(2)}, u32[]{:S(2)}) collective-permute-start(f32[3,2,16,256]{3,2,1,0:T(8,128)S(1)} %get-tuple-element.45), channel_id=1, source_target_pairs={{0,16},{16,0},{1,17},{17,1},{2,18},{18,2},{3,19},{19,3},{4,20},{20... | collective-permute-start | bytes 294920 | tf_op jit(solution)/shard_map/ppermute | solution.py:22
  120.0 4.6 %collective-permute-start.2 = (f32[3,2,16,256]{3,2,1,0:T(8,128)S(1)}, f32[3,2,16,256]{3,2,1,0:T(8,128)S(1)}, u32[]{:S(2)}, u32[]{:S(2)}) collective-permute-start(f32[3,2,16,256]{3,2,1,0:T(8,128)S(1)} %get-tuple-element.46), channel_id=1, source_target_pairs={{16,0},{0,16},{17,1},{1,17},{18,2},{2,18},{19,3},{3,19},{20,4},{4,... | collective-permute-start | bytes 294920 | tf_op jit(solution)/shard_map/ppermute | solution.py:24
  124.9 5.6 %collective-permute-start.3 = (f32[3,68,2,256]{3,2,1,0:T(2,128)S(1)}, f32[3,68,2,256]{3,2,1,0:T(2,128)S(1)}, u32[]{:S(2)}, u32[]{:S(2)}) collective-permute-start(f32[3,68,2,256]{3,2,1,0:T(2,128)S(1)} %get-tuple-element.25), channel_id=1, source_target_pairs={{1,0},{2,1},{3,2},{4,3},{5,4},{6,5},{7,6},{8,7},{9,8},{10,9},{11,1... | collective-permute-start | bytes 1253384 | tf_op jit(solution)/shard_map/ppermute | solution.py:24
  124.9 8.7 %collective-permute-start.4 = (f32[3,68,2,256]{3,2,1,0:T(2,128)S(1)}, f32[3,68,2,256]{3,2,1,0:T(2,128)S(1)}, u32[]{:S(2)}, u32[]{:S(2)}) collective-permute-start(f32[3,68,2,256]{3,2,1,0:T(2,128)S(1)} %get-tuple-element.26), channel_id=1, source_target_pairs={{0,1},{1,2},{2,3},{3,4},{4,5},{5,6},{6,7},{7,8},{8,9},{9,10},{10,1... | collective-permute-start | bytes 1253384 | tf_op jit(solution)/shard_map/ppermute | solution.py:22
  144.9 4.7 %collective-permute-start.5 = (f32[3,2,16,256]{3,2,1,0:T(8,128)S(1)}, f32[3,2,16,256]{3,2,1,0:T(8,128)S(1)}, u32[]{:S(2)}, u32[]{:S(2)}) collective-permute-start(f32[3,2,16,256]{3,2,1,0:T(8,128)S(1)} %get-tuple-element.40), channel_id=1, source_target_pairs={{0,16},{16,0},{1,17},{17,1},{2,18},{18,2},{3,19},{19,3},{4,20},{20... | collective-permute-start | bytes 294920 | tf_op jit(solution)/shard_map/ppermute | solution.py:22
  146.1 4.6 %collective-permute-start.6 = (f32[3,2,16,256]{3,2,1,0:T(8,128)S(1)}, f32[3,2,16,256]{3,2,1,0:T(8,128)S(1)}, u32[]{:S(2)}, u32[]{:S(2)}) collective-permute-start(f32[3,2,16,256]{3,2,1,0:T(8,128)S(1)} %get-tuple-element.41), channel_id=1, source_target_pairs={{16,0},{0,16},{17,1},{1,17},{18,2},{2,18},{19,3},{3,19},{20,4},{4,... | collective-permute-start | bytes 294920 | tf_op jit(solution)/shard_map/ppermute | solution.py:24
  150.7 10.3 %copy-start.3 = (f32[3,2,16,256]{3,2,1,0:T(8,128)}, f32[3,2,16,256]{3,2,1,0:T(8,128)S(1)}, u32[]{:S(2)}) copy-start(f32[3,2,16,256]{3,2,1,0:T(8,128)S(1)} %collective-permute-done.6) | copy-start | bytes 294916
  151.0 5.6 %collective-permute-start.7 = (f32[3,68,2,256]{3,2,1,0:T(2,128)S(1)}, f32[3,68,2,256]{3,2,1,0:T(2,128)S(1)}, u32[]{:S(2)}, u32[]{:S(2)}) collective-permute-start(f32[3,68,2,256]{3,2,1,0:T(2,128)S(1)} %get-tuple-element.21), channel_id=1, source_target_pairs={{1,0},{2,1},{3,2},{4,3},{5,4},{6,5},{7,6},{8,7},{9,8},{10,9},{11,1... | collective-permute-start | bytes 1253384 | tf_op jit(solution)/shard_map/ppermute | solution.py:24
  151.0 8.7 %collective-permute-start.8 = (f32[3,68,2,256]{3,2,1,0:T(2,128)S(1)}, f32[3,68,2,256]{3,2,1,0:T(2,128)S(1)}, u32[]{:S(2)}, u32[]{:S(2)}) collective-permute-start(f32[3,68,2,256]{3,2,1,0:T(2,128)S(1)} %get-tuple-element.22), channel_id=1, source_target_pairs={{0,1},{1,2},{2,3},{3,4},{4,5},{5,6},{6,7},{7,8},{8,9},{9,10},{10,1... | collective-permute-start | bytes 1253384 | tf_op jit(solution)/shard_map/ppermute | solution.py:22
  171.3 4.7 %collective-permute-start.10 = (f32[3,2,16,256]{3,2,1,0:T(8,128)S(1)}, f32[3,2,16,256]{3,2,1,0:T(8,128)S(1)}, u32[]{:S(2)}, u32[]{:S(2)}) collective-permute-start(f32[3,2,16,256]{3,2,1,0:T(8,128)S(1)} %get-tuple-element.36), channel_id=1, source_target_pairs={{16,0},{0,16},{17,1},{1,17},{18,2},{2,18},{19,3},{3,19},{20,4},{4,... | collective-permute-start | bytes 294920 | tf_op jit(solution)/shard_map/ppermute | solution.py:24
  172.6 4.6 %collective-permute-start.9 = (f32[3,2,16,256]{3,2,1,0:T(8,128)S(1)}, f32[3,2,16,256]{3,2,1,0:T(8,128)S(1)}, u32[]{:S(2)}, u32[]{:S(2)}) collective-permute-start(f32[3,2,16,256]{3,2,1,0:T(8,128)S(1)} %get-tuple-element.35), channel_id=1, source_target_pairs={{0,16},{16,0},{1,17},{17,1},{2,18},{18,2},{3,19},{19,3},{4,20},{20... | collective-permute-start | bytes 294920 | tf_op jit(solution)/shard_map/ppermute | solution.py:22
  177.2 10.3 %copy-start.4 = (f32[3,2,16,256]{3,2,1,0:T(8,128)}, f32[3,2,16,256]{3,2,1,0:T(8,128)S(1)}, u32[]{:S(2)}) copy-start(f32[3,2,16,256]{3,2,1,0:T(8,128)S(1)} %collective-permute-done.9) | copy-start | bytes 294916
  177.5 5.6 %collective-permute-start.11 = (f32[3,68,2,256]{3,2,1,0:T(2,128)S(1)}, f32[3,68,2,256]{3,2,1,0:T(2,128)S(1)}, u32[]{:S(2)}, u32[]{:S(2)}) collective-permute-start(f32[3,68,2,256]{3,2,1,0:T(2,128)S(1)} %get-tuple-element.17), channel_id=1, source_target_pairs={{1,0},{2,1},{3,2},{4,3},{5,4},{6,5},{7,6},{8,7},{9,8},{10,9},{11,1... | collective-permute-start | bytes 1253384 | tf_op jit(solution)/shard_map/ppermute | solution.py:24
  177.5 8.7 %collective-permute-start.12 = (f32[3,68,2,256]{3,2,1,0:T(2,128)S(1)}, f32[3,68,2,256]{3,2,1,0:T(2,128)S(1)}, u32[]{:S(2)}, u32[]{:S(2)}) collective-permute-start(f32[3,68,2,256]{3,2,1,0:T(2,128)S(1)} %get-tuple-element.18), channel_id=1, source_target_pairs={{0,1},{1,2},{2,3},{3,4},{4,5},{5,6},{6,7},{7,8},{8,9},{9,10},{10,1... | collective-permute-start | bytes 1253384 | tf_op jit(solution)/shard_map/ppermute | solution.py:22
  197.7 4.7 %collective-permute-start.13 = (f32[3,2,16,256]{3,2,1,0:T(8,128)S(1)}, f32[3,2,16,256]{3,2,1,0:T(8,128)S(1)}, u32[]{:S(2)}, u32[]{:S(2)}) collective-permute-start(f32[3,2,16,256]{3,2,1,0:T(8,128)S(1)} %get-tuple-element.30), channel_id=1, source_target_pairs={{0,16},{16,0},{1,17},{17,1},{2,18},{18,2},{3,19},{19,3},{4,20},{20... | collective-permute-start | bytes 294920 | tf_op jit(solution)/shard_map/ppermute | solution.py:22
  199.0 4.6 %collective-permute-start.14 = (f32[3,2,16,256]{3,2,1,0:T(8,128)S(1)}, f32[3,2,16,256]{3,2,1,0:T(8,128)S(1)}, u32[]{:S(2)}, u32[]{:S(2)}) collective-permute-start(f32[3,2,16,256]{3,2,1,0:T(8,128)S(1)} %get-tuple-element.31), channel_id=1, source_target_pairs={{16,0},{0,16},{17,1},{1,17},{18,2},{2,18},{19,3},{3,19},{20,4},{4,... | collective-permute-start | bytes 294920 | tf_op jit(solution)/shard_map/ppermute | solution.py:24
  203.9 5.6 %collective-permute-start.15 = (f32[3,68,2,256]{3,2,1,0:T(2,128)S(1)}, f32[3,68,2,256]{3,2,1,0:T(2,128)S(1)}, u32[]{:S(2)}, u32[]{:S(2)}) collective-permute-start(f32[3,68,2,256]{3,2,1,0:T(2,128)S(1)} %get-tuple-element.13), channel_id=1, source_target_pairs={{1,0},{2,1},{3,2},{4,3},{5,4},{6,5},{7,6},{8,7},{9,8},{10,9},{11,1... | collective-permute-start | bytes 1253384 | tf_op jit(solution)/shard_map/ppermute | solution.py:24
  204.0 8.7 %collective-permute-start.16 = (f32[3,68,2,256]{3,2,1,0:T(2,128)S(1)}, f32[3,68,2,256]{3,2,1,0:T(2,128)S(1)}, u32[]{:S(2)}, u32[]{:S(2)}) collective-permute-start(f32[3,68,2,256]{3,2,1,0:T(2,128)S(1)} %get-tuple-element.14), channel_id=1, source_target_pairs={{0,1},{1,2},{2,3},{3,4},{4,5},{5,6},{6,7},{7,8},{8,9},{9,10},{10,1... | collective-permute-start | bytes 1253384 | tf_op jit(solution)/shard_map/ppermute | solution.py:22
  218.1 2.4 %copy-start.5 = (f32[256,256,1,1]{1,0,3,2:T(8,128)S(1)}, f32[256,256,1,1]{1,0,3,2:T(8,128)}, u32[]{:S(2)}) copy-start(f32[256,256,1,1]{1,0,3,2:T(8,128)} %constant.40) | copy-start | bytes 786436
  (1 other events, 1.0 us)
